TPU v7x, 256 devices: a whole 4x4x8 slice. The times are simulated.
256 devices in a mesh: gx: 16 (over z_lo, x, core), gy: 4 (over y), tx: 4 (over z_hi).
Axes of the slice: x: 4, y: 4, z: 8 (z_hi: 4, z_lo: 2; z = z_hi * 2 + z_lo), core: 2. Of those that a mesh axis runs over, the one named last changes fastest.
Arguments:
- src_cell: int32 [8], P('tx'), may hold values from 0 to 524287
- basis: bfloat16 [16, 2, 3, 8, 128, 512], P('tx', None, None, None, 'gx', 'gy'), as said below
- images: bfloat16 [16, 2, 3, 8, 128, 512], P('tx', None, None, None, 'gx', 'gy'), as said below
- induction: bfloat16 [3, 8, 128, 512], P(None, 'tx', 'gx', 'gy'), may hold values from 0.25 to 4
Outputs:
- solution: float32 [8, 2, 3, 8, 128, 512], P('tx', None, None, None, 'gx', 'gy')
- residual: float32 [8, 2, 3, 8, 128, 512], P('tx', None, None, None, 'gx', 'gy')
Inputs may be any that keep to these rules, and one draw needn't show every extreme that they name: `basis`: entries of order one. `images`: entries of order one.
All inputs are finite; a program needn't handle non-finite values.
Results may differ from a plain program's by a relative error of at most 0.0003.
Values may be sent and summed in bfloat16 or wider, within the bound.
No kernel may reach another device: no remote copies, remote signals or barrier semaphores. Data moves between devices by JAX's collectives and lax.ppermute only.
A program may use at most 64 MiB of HBM per device.

v0:
```python
import jax
import jax.numpy as jnp
from jax import lax
from jax.sharding import PartitionSpec as P

CYCLES = 2
ARNOLDI = 2
eps = 1e-06


def with_halo(x, sides, width):
    for axis, dim in sides:
        size, length = (lax.axis_size(axis), x.shape[dim])
        up = [(i, (i + 1) % size) for i in range(size - 1)]
        down = [(j, i) for i, j in up]
        last = lax.slice_in_dim(x, length - width, length, axis=dim)
        initial = lax.slice_in_dim(x, 0, width, axis=dim)
        before = lax.ppermute(last, axis, up)
        after = lax.ppermute(initial, axis, down)
        x = jnp.concatenate([before, x, after], axis=dim)
    return x


def differ(field, axis, forward):
    axis = field.ndim + axis
    count = field.shape[axis]
    delta = lax.slice_in_dim(field, 1, count, axis=axis) - lax.slice_in_dim(
        field, 0, count - 1, axis=axis
    )
    zero = jnp.zeros_like(lax.slice_in_dim(field, 0, 1, axis=axis))
    if forward:
        return jnp.concatenate([delta, zero], axis=axis)
    return jnp.concatenate([zero, delta], axis=axis)


def curl_curl(padded):
    e_x = padded[..., 0, :, :, :]
    e_y = padded[..., 1, :, :, :]
    e_z = padded[..., 2, :, :, :]
    b_x = differ(e_z, -1, True) - differ(e_y, -3, True)
    b_y = differ(e_x, -3, True) - differ(e_z, -2, True)
    b_z = differ(e_y, -2, True) - differ(e_x, -1, True)
    c_x = differ(b_z, -1, False) - differ(b_y, -3, False)
    c_y = differ(b_x, -3, False) - differ(b_z, -2, False)
    c_z = differ(b_y, -2, False) - differ(b_x, -1, False)
    whole = jnp.stack([c_x, c_y, c_z], axis=-4)
    return whole[..., 1:-1, 1:-1, 1:-1]


def apply_operator(field, induct):
    framed = with_halo(field, (("gx", 4), ("gy", 5)), 1)
    padded = jnp.pad(framed, [(0, 0), (0, 0), (0, 0), (1, 1), (0, 0), (0, 0)])
    curled = curl_curl(padded)
    real_part = curled[:, 0] - induct[None] * field[:, 1]
    imag_part = curled[:, 1] + induct[None] * field[:, 0]
    return jnp.stack([real_part, imag_part], axis=1)


def source_field(cells, z_pos, x_pos, y_pos, size_x, size_y, induct):
    plane = size_x * size_y
    src_z = cells // plane
    rest = cells % plane
    src_x = rest // size_y
    src_y = rest % size_y
    d_z = (z_pos[None, :] - src_z[:, None]).astype(jnp.float32)
    d_x = (x_pos[None, :] - src_x[:, None]).astype(jnp.float32)
    d_y = (y_pos[None, :] - src_y[:, None]).astype(jnp.float32)
    dist = jnp.sqrt(
        d_z[:, :, None, None] ** 2 + d_x[:, None, :, None] ** 2 + d_y[:, None, None, :] ** 2
    )
    primary = jnp.exp(-dist / ((size_x + size_y) / 8.0))
    weights = jnp.array([1.0, 0.5, 0.25], dtype=jnp.float32)
    real_part = (induct - 1.0)[None] * weights[None, :, None, None, None] * primary[:, None]
    return jnp.stack([real_part, 0.5 * real_part], axis=1)


def inner_basis(vectors, field):
    return jnp.einsum(
        "kpczxy,spczxy->ks",
        vectors,
        field,
        precision=lax.Precision.HIGHEST,
        preferred_element_type=jnp.float32,
    )


def combine(coeffs, vectors):
    return jnp.einsum(
        "ks,kpczxy->spczxy",
        coeffs,
        vectors,
        precision=lax.Precision.HIGHEST,
        preferred_element_type=jnp.float32,
    )


def per_source(left, right):
    return jnp.sum(left * right, axis=(1, 2, 3, 4, 5))


def expand(values):
    return values[:, None, None, None, None, None]


def small_solve(matrix, rhs):
    factor = jnp.linalg.cholesky(matrix)
    return jax.scipy.linalg.cho_solve((factor, True), rhs)


def on_device(src_cell, basis, images, induction):
    all_basis, all_images, gathered = (
        lax.all_gather(basis, "tx", axis=0, tiled=True),
        lax.all_gather(images, "tx", axis=0, tiled=True),
        lax.all_gather(induction, "tx", axis=1, tiled=True),
    )
    induct = gathered.astype(jnp.float32)
    depth = basis.shape[3]
    width_x = basis.shape[4]
    width_y = basis.shape[5]
    size_x = width_x * lax.axis_size("gx")
    size_y = width_y * lax.axis_size("gy")
    z_pos = jnp.arange(depth, dtype=jnp.int32)
    x_pos = lax.axis_index("gx") * width_x + jnp.arange(width_x, dtype=jnp.int32)
    y_pos = lax.axis_index("gy") * width_y + jnp.arange(width_y, dtype=jnp.int32)
    rhs = source_field(src_cell, z_pos, x_pos, y_pos, size_x, size_y, induct)
    gram_part = jnp.einsum(
        "kpczxy,lpczxy->kl", all_images, all_images, preferred_element_type=jnp.float32
    )
    gram, start_inner = lax.psum((gram_part, inner_basis(all_images, rhs)), ("gx", "gy"))
    factor = jnp.linalg.cholesky(gram)
    h_zero = jax.scipy.linalg.cho_solve((factor, True), start_inner)
    residual = rhs - combine(h_zero, all_images)
    solution = combine(h_zero, all_basis)
    for cycle in range(CYCLES):
        beta = jnp.sqrt(lax.psum(per_source(residual, residual), ("gx", "gy")) + eps)
        krylov = [residual / expand(beta)]
        h_cols = []
        g_cols = []
        for step in range(ARNOLDI):
            work = apply_operator(krylov[step], induct)
            g_raw = lax.psum(inner_basis(all_images, work), ("gx", "gy"))
            g_now = jax.scipy.linalg.cho_solve((factor, True), g_raw)
            work = work - combine(g_now, all_images)
            h_now = lax.psum(jnp.stack([per_source(vec, work) for vec in krylov]), ("gx", "gy"))
            for index in range(step + 1):
                work = work - expand(h_now[index]) * krylov[index]
            h_next = jnp.sqrt(lax.psum(per_source(work, work), ("gx", "gy")) + eps)
            krylov.append(work / expand(h_next))
            pad_rows = jnp.zeros((ARNOLDI - step - 1, h_next.shape[0]), dtype=jnp.float32)
            h_cols.append(jnp.concatenate([h_now, h_next[None], pad_rows], axis=0))
            g_cols.append(g_now)
        hess = jnp.stack(h_cols, axis=1)
        g_all = jnp.stack(g_cols, axis=1)
        normal = jnp.einsum("ijs,iks->sjk", hess, hess, precision=lax.Precision.HIGHEST)
        target = beta[:, None] * jnp.transpose(hess[0])
        y_coef = jax.vmap(small_solve)(normal, target)
        update = expand(y_coef[:, 0]) * krylov[0]
        step = 1
        update = update + expand(y_coef[:, step]) * krylov[step]
        u_coef = jnp.einsum("kjs,sj->ks", g_all, y_coef, precision=lax.Precision.HIGHEST)
        solution = solution + update - combine(u_coef, all_basis)
        first = jnp.zeros((ARNOLDI + 1, beta.shape[0]), dtype=jnp.float32).at[0].set(beta)
        t_coef = first - jnp.einsum("ijs,sj->is", hess, y_coef, precision=lax.Precision.HIGHEST)
        residual = expand(t_coef[0]) * krylov[0]
        for index in range(1, ARNOLDI + 1):
            residual = residual + expand(t_coef[index]) * krylov[index]
    return (solution, residual)


def solution(mesh):
    in_specs = (
        P("tx"),
        P("tx", None, None, None, "gx", "gy"),
        P("tx", None, None, None, "gx", "gy"),
        P(None, "tx", "gx", "gy"),
    )
    out_specs = (P("tx", None, None, None, "gx", "gy"), P("tx", None, None, None, "gx", "gy"))
    return jax.shard_map(
        on_device, mesh=mesh, in_specs=in_specs, out_specs=out_specs, check_vma=False
    )
```

profile of v0, /device:TPU:40, one launch (start us, length us, event | category | flops | bytes accessed | tf_op | source)
XLA Modules:
  0.0 2366.0 jit_solution(5453150176349590648)
XLA Ops:
  7.9 16.6 all_gather.10
  26.5 26.6 %all-gather.3.cloned.1.call-done = bf16[16,2,3,8,8,128]{5,4,3,2,1,0:T(8,128)(2,1)} async-done(((bf16[4,2,3,8,8,128]{5,4,3,2,1,0:T(8,128)(2,1)}), bf16[16,2,3,8,8,128]{5,4,3,2,1,0:T(8,128)(2,1)}) %all-gather.3.cloned.1.call-update) | async-done | bytes 1572880 | tf_op jit(solution)/shard_map/all_gather | solution.py:113
  53.1 5.4 convolution_bitcast_fusion
  62.2 144.3 %all-reduce.54 = (f32[16,2]{0,1:T(2,128)S(1)}, f32[16,16]{0,1:T(8,128)S(1)}) all-reduce(f32[16,2]{0,1:T(2,128)S(1)} %convolution_bitcast_fusion.8, f32[16,16]{0,1:T(8,128)S(1)} %convolution_bitcast_fusion), channel_id=1, replica_groups=mesh['gx'=16,'gy'=4,'tx'=4] {'gx','gy'}, use_global_device_ids=true, to_apply=%region_3.4 | all-reduce | flops 288 | bytes 2304 | tf_op jit(solution)/shard_map/psum | solution.py:129
  214.2 143.8 %psum.114 = f32[2]{0:T(128)S(1)} all-reduce(f32[2]{0:T(128)S(1)} %get-tuple-element.119), channel_id=1, replica_groups=mesh['gx'=16,'gy'=4,'tx'=4] {'gx','gy'}, use_global_device_ids=true, to_apply=%region_5.7 | all-reduce | flops 2 | bytes 16 | tf_op jit(solution)/shard_map/psum | solution.py:135
  360.2 5.8 collective-permute-start.1
  394.9 140.9 %psum.115 = f32[16,2]{0,1:T(2,128)S(1)} all-reduce(f32[16,2]{0,1:T(2,128)S(1)} %convolution_bitcast_fusion.7), channel_id=1, replica_groups=mesh['gx'=16,'gy'=4,'tx'=4] {'gx','gy'}, use_global_device_ids=true, to_apply=%region_6.8 | all-reduce | flops 32 | bytes 256 | tf_op jit(solution)/shard_map/psum | solution.py:141
  539.4 139.6 %psum.116 = f32[1,2]{1,0:T(1,128)S(1)} all-reduce(f32[1,2]{1,0:T(1,128)S(1)} %bitcast.337), channel_id=1, replica_groups=mesh['gx'=16,'gy'=4,'tx'=4] {'gx','gy'}, use_global_device_ids=true, to_apply=%region_8.10 | all-reduce | flops 2 | bytes 16 | tf_op jit(solution)/shard_map/psum | solution.py:144
  679.7 139.5 %psum.117 = f32[2]{0:T(128)S(1)} all-reduce(f32[2]{0:T(128)S(1)} %get-tuple-element.49), channel_id=1, replica_groups=mesh['gx'=16,'gy'=4,'tx'=4] {'gx','gy'}, use_global_device_ids=true, to_apply=%region_10.12 | all-reduce | flops 2 | bytes 16 | tf_op jit(solution)/shard_map/psum | solution.py:147
  821.4 5.8 collective-permute-start.5
  835.6 4.9 collective-permute-done.6
  856.1 141.1 %psum.118 = f32[16,2]{0,1:T(2,128)S(1)} all-reduce(f32[16,2]{0,1:T(2,128)S(1)} %convolution_bitcast_fusion.6), channel_id=1, replica_groups=mesh['gx'=16,'gy'=4,'tx'=4] {'gx','gy'}, use_global_device_ids=true, to_apply=%region_11.13 | all-reduce | flops 32 | bytes 256 | tf_op jit(solution)/shard_map/psum | solution.py:141
  1000.9 139.0 %psum.119 = f32[2,2]{1,0:T(2,128)S(1)} all-reduce(f32[2,2]{1,0:T(2,128)S(1)} %pad_maximum_fusion.26), channel_id=1, replica_groups=mesh['gx'=16,'gy'=4,'tx'=4] {'gx','gy'}, use_global_device_ids=true, to_apply=%region_14.16 | all-reduce | flops 4 | bytes 32 | tf_op jit(solution)/shard_map/psum | solution.py:144
  1140.6 140.2 %psum.120 = f32[2]{0:T(128)S(1)} all-reduce(f32[2]{0:T(128)S(1)} %get-tuple-element.47), channel_id=1, replica_groups=mesh['gx'=16,'gy'=4,'tx'=4] {'gx','gy'}, use_global_device_ids=true, to_apply=%region_16.18 | all-reduce | flops 2 | bytes 16 | tf_op jit(solution)/shard_map/psum | solution.py:147
  1283.8 139.0 %psum.121 = f32[2]{0:T(128)S(1)} all-reduce(f32[2]{0:T(128)S(1)} %get-tuple-element.45), channel_id=1, replica_groups=mesh['gx'=16,'gy'=4,'tx'=4] {'gx','gy'}, use_global_device_ids=true, to_apply=%region_20.24 | all-reduce | flops 2 | bytes 16 | tf_op jit(solution)/shard_map/psum | solution.py:135
  1425.0 5.8 collective-permute-start.9
  1441.5 5.5 collective-permute-done.10
  1462.7 140.7 %psum.122 = f32[16,2]{0,1:T(2,128)S(1)} all-reduce(f32[16,2]{0,1:T(2,128)S(1)} %convolution_bitcast_fusion.5), channel_id=1, replica_groups=mesh['gx'=16,'gy'=4,'tx'=4] {'gx','gy'}, use_global_device_ids=true, to_apply=%region_21.25 | all-reduce | flops 32 | bytes 256 | tf_op jit(solution)/shard_map/psum | solution.py:141
  1607.0 138.7 %psum.123 = f32[1,2]{1,0:T(1,128)S(1)} all-reduce(f32[1,2]{1,0:T(1,128)S(1)} %bitcast.338), channel_id=1, replica_groups=mesh['gx'=16,'gy'=4,'tx'=4] {'gx','gy'}, use_global_device_ids=true, to_apply=%region_23.27 | all-reduce | flops 2 | bytes 16 | tf_op jit(solution)/shard_map/psum | solution.py:144
  1746.3 140.5 %psum.124 = f32[2]{0:T(128)S(1)} all-reduce(f32[2]{0:T(128)S(1)} %get-tuple-element.43), channel_id=1, replica_groups=mesh['gx'=16,'gy'=4,'tx'=4] {'gx','gy'}, use_global_device_ids=true, to_apply=%region_25.29 | all-reduce | flops 2 | bytes 16 | tf_op jit(solution)/shard_map/psum | solution.py:147
  1889.0 5.8 collective-permute-start.13
  1923.7 140.9 %psum.125 = f32[16,2]{0,1:T(2,128)S(1)} all-reduce(f32[16,2]{0,1:T(2,128)S(1)} %convolution_bitcast_fusion.4), channel_id=1, replica_groups=mesh['gx'=16,'gy'=4,'tx'=4] {'gx','gy'}, use_global_device_ids=true, to_apply=%region_26.30 | all-reduce | flops 32 | bytes 256 | tf_op jit(solution)/shard_map/psum | solution.py:141
  2068.3 139.0 %psum.126 = f32[2,2]{1,0:T(2,128)S(1)} all-reduce(f32[2,2]{1,0:T(2,128)S(1)} %pad_maximum_fusion.27), channel_id=1, replica_groups=mesh['gx'=16,'gy'=4,'tx'=4] {'gx','gy'}, use_global_device_ids=true, to_apply=%region_29.33 | all-reduce | flops 4 | bytes 32 | tf_op jit(solution)/shard_map/psum | solution.py:144
  2208.7 140.2 %psum.127 = f32[2]{0:T(128)S(1)} all-reduce(f32[2]{0:T(128)S(1)} %get-tuple-element.41), channel_id=1, replica_groups=mesh['gx'=16,'gy'=4,'tx'=4] {'gx','gy'}, use_global_device_ids=true, to_apply=%region_31.35 | all-reduce | flops 2 | bytes 16 | tf_op jit(solution)/shard_map/psum | solution.py:147
  (249 shorter events, 161.1 us)
Async XLA Ops:
  7.2 46.0 %all-gather.3.cloned.1.call-start = ((), (), s32[]{:S(2)}) async-start(), calls=%async_computation | async-start | bytes 1966080 | tf_op jit(solution)/shard_map/all_gather | solution.py:113
  7.9 1422.9 %all-gather.5.cloned.1.call-start = ((), (), s32[]{:S(2)}) async-start(), calls=%async_computation.1 | async-start | bytes 1966080 | tf_op jit(solution)/shard_map/all_gather | solution.py:112
  53.1 5.4 copy-start.1
  358.2 7.7 collective-permute-start
  360.2 7.5 collective-permute-start.1
  368.5 10.8 collective-permute-start.2
  370.4 10.8 collective-permute-start.3
  389.8 1.4 copy-start.2
  819.5 7.8 collective-permute-start.4
  821.4 7.5 collective-permute-start.5
  829.7 10.8 collective-permute-start.6
  831.6 10.8 collective-permute-start.7
  851.0 1.4 copy-start.3
  1423.1 11.5 collective-permute-start.8
  1425.0 9.5 collective-permute-start.9
  1435.4 11.7 collective-permute-start.10
  1437.3 11.7 collective-permute-start.11
  1457.6 1.4 copy-start.4
  1887.0 7.8 collective-permute-start.12
  1889.0 7.5 collective-permute-start.13
  1897.3 10.8 collective-permute-start.14
  1899.2 10.8 collective-permute-start.15
  1918.6 1.4 copy-start.5
  2349.7 4.0 copy-start
Sparse Core Ops, SparseCore 0:
  9.8 43.2 all-gather.2
  366.1 35.2 all-gather.4
where the time goes:
time: 2380 us; the launch traced here: 2370 us
  blocking collectives  2120 us (89%)
  waiting for transfers between devices  59.9 us (3%)
  starting transfers between devices  54.6 us (2%)
  matrix products  50.6 us (2%)
  other arithmetic  50.3 us (2%)
    psum x4, blocking collectives, on_device(): g_raw = lax.psum(inner_basis(all_images, work), ('gx', 'gy'))  564 us
    psum x4, blocking collectives, on_device(): h_next = jnp.sqrt(lax.psum(per_source(work, work), ('gx', 'gy')) + eps)  560 us
    psum x4, blocking collectives, on_device(): lax.psum(jnp.stack([per_source(vec, work) for vec in krylov]), ('gx', 'gy'))  556 us
    psum x2, blocking collectives, on_device(): lax.psum(per_source(residual, residual), ('gx', 'gy')) + eps  283 us
    psum x1, blocking collectives, on_device(): lax.psum((gram_part, inner_basis(all_images, rhs)), ('gx', 'gy'))  144 us
  transfers between devices with their start and end apart: 18, of which 12 were waited for; matrix products, arithmetic and copies ran while one was open for 2% of the time, Pallas kernels for 0%

commit v1 on v0

--- a/solution.py
+++ b/solution.py
@@ -126,7 +126,7 @@
     gram_part = jnp.einsum(
         "kpczxy,lpczxy->kl", all_images, all_images, preferred_element_type=jnp.float32
     )
-    gram, start_inner = lax.psum((gram_part, inner_basis(all_images, rhs)), ("gx", "gy"))
+    gram, start_inner = lax.psum(lax.psum((gram_part, inner_basis(all_images, rhs)), "gy"), "gx")
     factor = jnp.linalg.cholesky(gram)
     h_zero = jax.scipy.linalg.cho_solve((factor, True), start_inner)
     residual = rhs - combine(h_zero, all_images)

time: 2380 us -> 2270 us (0.954)
  blocking collectives: 2120 us -> 2020 us
    psum x1 -> x2, blocking collectives: 144 us -> 39.3 us  [the longest x1 30.6 us: on_device(): lax.psum(lax.psum((gram_part, inner_basis(all_images, rhs)), 'gy'), 'gx')]
where the time goes in v1:
time: 2270 us; the launch traced here: 2260 us
  blocking collectives  2020 us (89%)
  waiting for transfers between devices  59.9 us (3%)
  starting transfers between devices  54.6 us (2%)
  matrix products  50.6 us (2%)
  other arithmetic  50.3 us (2%)
    psum x4, blocking collectives, on_device(): g_raw = lax.psum(inner_basis(all_images, work), ('gx', 'gy'))  564 us
    psum x4, blocking collectives, on_device(): h_next = jnp.sqrt(lax.psum(per_source(work, work), ('gx', 'gy')) + eps)  560 us
    psum x4, blocking collectives, on_device(): lax.psum(jnp.stack([per_source(vec, work) for vec in krylov]), ('gx', 'gy'))  556 us
    psum x2, blocking collectives, on_device(): lax.psum(per_source(residual, residual), ('gx', 'gy')) + eps  280 us
  transfers between devices with their start and end apart: 18, of which 12 were waited for; matrix products, arithmetic and copies ran while one was open for 2% of the time, Pallas kernels for 0%

profile of v1, /device:TPU:40, one launch (start us, length us, event | category | flops | bytes accessed | tf_op | source)
XLA Modules:
  0.0 2258.2 jit_solution(12443816655771074573)
XLA Ops:
  7.9 16.6 all_gather.10
  26.5 26.6 %all-gather.3.cloned.1.call-done = bf16[16,2,3,8,8,128]{5,4,3,2,1,0:T(8,128)(2,1)} async-done(((bf16[4,2,3,8,8,128]{5,4,3,2,1,0:T(8,128)(2,1)}), bf16[16,2,3,8,8,128]{5,4,3,2,1,0:T(8,128)(2,1)}) %all-gather.3.cloned.1.call-update) | async-done | bytes 1572880 | tf_op jit(solution)/shard_map/all_gather | solution.py:113
  53.1 5.4 convolution_bitcast_fusion
  62.2 8.7 all-reduce.55
  70.9 30.6 %all-reduce.54 = (f32[16,2]{0,1:T(2,128)S(1)}, f32[16,16]{0,1:T(8,128)S(1)}) all-reduce(f32[16,2]{0,1:T(2,128)S(1)} %get-tuple-element.41, f32[16,16]{0,1:T(8,128)S(1)} %get-tuple-element.42), channel_id=1, replica_groups=mesh['gx'=16,'gy'=4,'tx'=4] {'gx'}, use_global_device_ids=true, to_apply=%region_5.6 | all-reduce | flops 288 | bytes 2304 | tf_op jit(solution)/shard_map/psum | solution.py:129
  109.1 141.1 %psum.130 = f32[2]{0:T(128)S(1)} all-reduce(f32[2]{0:T(128)S(1)} %get-tuple-element.121), channel_id=1, replica_groups=mesh['gx'=16,'gy'=4,'tx'=4] {'gx','gy'}, use_global_device_ids=true, to_apply=%region_7.9 | all-reduce | flops 2 | bytes 16 | tf_op jit(solution)/shard_map/psum | solution.py:135
  252.4 5.8 collective-permute-start.1
  287.1 140.9 %psum.131 = f32[16,2]{0,1:T(2,128)S(1)} all-reduce(f32[16,2]{0,1:T(2,128)S(1)} %convolution_bitcast_fusion.7), channel_id=1, replica_groups=mesh['gx'=16,'gy'=4,'tx'=4] {'gx','gy'}, use_global_device_ids=true, to_apply=%region_8.10 | all-reduce | flops 32 | bytes 256 | tf_op jit(solution)/shard_map/psum | solution.py:141
  431.6 139.6 %psum.132 = f32[1,2]{1,0:T(1,128)S(1)} all-reduce(f32[1,2]{1,0:T(1,128)S(1)} %bitcast.337), channel_id=1, replica_groups=mesh['gx'=16,'gy'=4,'tx'=4] {'gx','gy'}, use_global_device_ids=true, to_apply=%region_10.12 | all-reduce | flops 2 | bytes 16 | tf_op jit(solution)/shard_map/psum | solution.py:144
  571.9 139.5 %psum.133 = f32[2]{0:T(128)S(1)} all-reduce(f32[2]{0:T(128)S(1)} %get-tuple-element.51), channel_id=1, replica_groups=mesh['gx'=16,'gy'=4,'tx'=4] {'gx','gy'}, use_global_device_ids=true, to_apply=%region_12.14 | all-reduce | flops 2 | bytes 16 | tf_op jit(solution)/shard_map/psum | solution.py:147
  713.6 5.8 collective-permute-start.5
  748.3 141.1 %psum.134 = f32[16,2]{0,1:T(2,128)S(1)} all-reduce(f32[16,2]{0,1:T(2,128)S(1)} %convolution_bitcast_fusion.6), channel_id=1, replica_groups=mesh['gx'=16,'gy'=4,'tx'=4] {'gx','gy'}, use_global_device_ids=true, to_apply=%region_13.15 | all-reduce | flops 32 | bytes 256 | tf_op jit(solution)/shard_map/psum | solution.py:141
  893.1 139.0 %psum.135 = f32[2,2]{1,0:T(2,128)S(1)} all-reduce(f32[2,2]{1,0:T(2,128)S(1)} %pad_maximum_fusion.26), channel_id=1, replica_groups=mesh['gx'=16,'gy'=4,'tx'=4] {'gx','gy'}, use_global_device_ids=true, to_apply=%region_16.18 | all-reduce | flops 4 | bytes 32 | tf_op jit(solution)/shard_map/psum | solution.py:144
  1032.9 140.2 %psum.136 = f32[2]{0:T(128)S(1)} all-reduce(f32[2]{0:T(128)S(1)} %get-tuple-element.49), channel_id=1, replica_groups=mesh['gx'=16,'gy'=4,'tx'=4] {'gx','gy'}, use_global_device_ids=true, to_apply=%region_18.20 | all-reduce | flops 2 | bytes 16 | tf_op jit(solution)/shard_map/psum | solution.py:147
  1176.0 139.0 %psum.137 = f32[2]{0:T(128)S(1)} all-reduce(f32[2]{0:T(128)S(1)} %get-tuple-element.47), channel_id=1, replica_groups=mesh['gx'=16,'gy'=4,'tx'=4] {'gx','gy'}, use_global_device_ids=true, to_apply=%region_22.26 | all-reduce | flops 2 | bytes 16 | tf_op jit(solution)/shard_map/psum | solution.py:135
  1317.3 5.8 collective-permute-start.9
  1333.8 5.5 collective-permute-done.10
  1354.9 140.7 %psum.138 = f32[16,2]{0,1:T(2,128)S(1)} all-reduce(f32[16,2]{0,1:T(2,128)S(1)} %convolution_bitcast_fusion.5), channel_id=1, replica_groups=mesh['gx'=16,'gy'=4,'tx'=4] {'gx','gy'}, use_global_device_ids=true, to_apply=%region_23.27 | all-reduce | flops 32 | bytes 256 | tf_op jit(solution)/shard_map/psum | solution.py:141
  1499.2 138.7 %psum.139 = f32[1,2]{1,0:T(1,128)S(1)} all-reduce(f32[1,2]{1,0:T(1,128)S(1)} %bitcast.338), channel_id=1, replica_groups=mesh['gx'=16,'gy'=4,'tx'=4] {'gx','gy'}, use_global_device_ids=true, to_apply=%region_25.29 | all-reduce | flops 2 | bytes 16 | tf_op jit(solution)/shard_map/psum | solution.py:144
  1638.5 140.5 %psum.140 = f32[2]{0:T(128)S(1)} all-reduce(f32[2]{0:T(128)S(1)} %get-tuple-element.45), channel_id=1, replica_groups=mesh['gx'=16,'gy'=4,'tx'=4] {'gx','gy'}, use_global_device_ids=true, to_apply=%region_27.31 | all-reduce | flops 2 | bytes 16 | tf_op jit(solution)/shard_map/psum | solution.py:147
  1781.2 5.8 collective-permute-start.13
  1815.9 140.9 %psum.141 = f32[16,2]{0,1:T(2,128)S(1)} all-reduce(f32[16,2]{0,1:T(2,128)S(1)} %convolution_bitcast_fusion.4), channel_id=1, replica_groups=mesh['gx'=16,'gy'=4,'tx'=4] {'gx','gy'}, use_global_device_ids=true, to_apply=%region_28.32 | all-reduce | flops 32 | bytes 256 | tf_op jit(solution)/shard_map/psum | solution.py:141
  1960.6 139.0 %psum.142 = f32[2,2]{1,0:T(2,128)S(1)} all-reduce(f32[2,2]{1,0:T(2,128)S(1)} %pad_maximum_fusion.27), channel_id=1, replica_groups=mesh['gx'=16,'gy'=4,'tx'=4] {'gx','gy'}, use_global_device_ids=true, to_apply=%region_31.35 | all-reduce | flops 4 | bytes 32 | tf_op jit(solution)/shard_map/psum | solution.py:144
  2101.0 140.2 %psum.143 = f32[2]{0:T(128)S(1)} all-reduce(f32[2]{0:T(128)S(1)} %get-tuple-element.43), channel_id=1, replica_groups=mesh['gx'=16,'gy'=4,'tx'=4] {'gx','gy'}, use_global_device_ids=true, to_apply=%region_33.37 | all-reduce | flops 2 | bytes 16 | tf_op jit(solution)/shard_map/psum | solution.py:147
  (250 shorter events, 166.0 us)
Async XLA Ops:
  7.2 46.0 %all-gather.3.cloned.1.call-start = ((), (), s32[]{:S(2)}) async-start(), calls=%async_computation | async-start | bytes 1966080 | tf_op jit(solution)/shard_map/all_gather | solution.py:113
  7.9 1315.2 %all-gather.5.cloned.1.call-start = ((), (), s32[]{:S(2)}) async-start(), calls=%async_computation.1 | async-start | bytes 1966080 | tf_op jit(solution)/shard_map/all_gather | solution.py:112
  53.1 5.4 copy-start.1
  250.5 7.7 collective-permute-start
  252.4 7.5 collective-permute-start.1
  260.7 10.8 collective-permute-start.2
  262.6 10.8 collective-permute-start.3
  282.1 1.4 copy-start.2
  711.7 7.8 collective-permute-start.4
  713.6 7.5 collective-permute-start.5
  721.9 10.8 collective-permute-start.6
  723.9 10.8 collective-permute-start.7
  743.3 1.4 copy-start.3
  1315.4 11.5 collective-permute-start.8
  1317.3 9.5 collective-permute-start.9
  1327.6 11.7 collective-permute-start.10
  1329.6 11.7 collective-permute-start.11
  1349.8 1.4 copy-start.4
  1779.3 7.8 collective-permute-start.12
  1781.2 7.5 collective-permute-start.13
  1789.5 10.8 collective-permute-start.14
  1791.4 10.8 collective-permute-start.15
  1810.8 1.4 copy-start.5
  2241.9 4.0 copy-start
Sparse Core Ops, SparseCore 0:
  9.8 43.2 all-gather.2
  258.3 35.2 all-gather.4
